TPU v7x, 512 devices: a whole 4x4x16 slice. The times are simulated.
512 devices in a mesh: param: 16 (over y, x), dom: 32 (over z, core).
Axes of the slice: x: 4, y: 4, z: 16, core: 2. Of those that a mesh axis runs over, the one named last changes fastest.
Arguments:
- particles: bfloat16 [512, 524288], P('dom', 'param'), may hold values from -40 to 40
- scores: bfloat16 [512, 524288], P('dom', 'param'), may hold values from -6 to 6
- basis: bfloat16 [524288, 128], P(('param', 'dom')), may hold values from -0.0078125 to 0.0078125
Outputs:
- velocity: bfloat16 [512, 524288], P('dom', 'param')
- phi: float32 [512, 128], P('dom')
All inputs are finite; a program needn't handle non-finite values.
Results may differ from a plain program's by a relative error of at most 0.0049.
Values may be sent and summed in bfloat16 or wider, within the bound.
No kernel may reach another device: no remote copies, remote signals or barrier semaphores. Data moves between devices by JAX's collectives and lax.ppermute only.
A program may use at most 64 MiB of HBM per device.

v0:
```python
import math
import jax
import jax.numpy as jnp
from jax import lax
from jax.sharding import PartitionSpec as P

P_SIZE = 524288
R = 128


def sent_to_all(array, axis):
    peers = lax.axis_size(axis)
    return lax.all_to_all(
        jnp.broadcast_to(array[None], (peers, *array.shape)), axis, 0, 0, tiled=True
    )


def of_everyone(array, axis):
    return sent_to_all(array, axis).sum(axis=0)


def in_one(arrays, axis):
    ends = [0]
    for a in arrays:
        ends.append(ends[-1] + a.size)
    total = of_everyone(jnp.concatenate([a.ravel() for a in arrays]), axis)
    return tuple((total[b:e].reshape(a.shape) for a, b, e in zip(arrays, ends, ends[1:])))


def in_one_piece(arrays, axis, dim, along):
    widths = [a.shape[along] for a in arrays]
    both = jnp.concatenate(arrays, axis=along)
    result = lax.all_gather(both, axis, axis=dim, tiled=True)
    return tuple(jnp.split(result, [sum(widths[:k]) for k in range(1, len(widths))], axis=along))


def stein_terms(own, every, every_score):
    count = every.shape[0]
    every_sq = jnp.sum(every * every, axis=1)
    own_sq = jnp.sum(own * own, axis=1)
    center = jnp.mean(every, axis=0)
    width = 2.0 * (jnp.mean(every_sq) - jnp.sum(center * center)) / math.log(count) + 1e-06
    cross = jnp.dot(own, every.T, precision=lax.Precision.HIGHEST)
    dist = own_sq[:, None] + every_sq[None, :] - 2.0 * cross
    kern = jnp.exp(-dist / width)
    drive = jnp.dot(kern, every_score, precision=lax.Precision.HIGHEST)
    pull = jnp.dot(kern, every, precision=lax.Precision.HIGHEST)
    total = jnp.sum(kern, axis=1)
    return (drive + 2.0 / width * (own * total[:, None] - pull)) / count


def lift_rows(phi_rows, basis_rows):
    lifted = lax.dot_general(
        phi_rows.astype(jnp.bfloat16),
        basis_rows,
        (((1,), (1,)), ((), ())),
        preferred_element_type=jnp.float32,
    )
    return (lifted * math.sqrt(P_SIZE / R)).astype(jnp.bfloat16)


def body(particles, scores, basis):
    rows = particles.shape[0]
    first = lax.axis_index("dom") * rows
    block_basis = lax.all_gather(basis, "dom", axis=0, tiled=True)
    partial_c = jnp.dot(particles, block_basis, preferred_element_type=jnp.float32)
    partial_s = jnp.dot(scores, block_basis, preferred_element_type=jnp.float32)
    summed_c, summed_s = in_one((partial_c, partial_s), "param")
    every, every_score = in_one_piece((summed_c, summed_s), "dom", 0, 1)
    own = lax.dynamic_slice_in_dim(every, first, rows, 0)
    phi = stein_terms(own, every, every_score)
    velocity = lift_rows(phi, block_basis)
    return (velocity, phi)


def solution(mesh):
    in_specs = (P("dom", "param"), P("dom", "param"), P(("param", "dom"), None))
    out_specs = (P("dom", "param"), P("dom", None))
    return jax.shard_map(body, mesh=mesh, in_specs=in_specs, out_specs=out_specs, check_vma=False)
```

profile of v0, /device:TPU:1, one launch (start us, length us, event | category | flops | bytes accessed | tf_op | source)
XLA Modules:
  0.0 167.6 jit_solution(8513275402666287345)
XLA Ops:
  7.2 0.0 copy-start
  7.2 0.0 all-gather.2.cloned.1.call-start
  7.2 0.7 all-gather.2.cloned.1.call-update
  7.9 0.0 copy-start.2
  7.9 87.5 %all-gather.2.cloned.1.call-done = bf16[32768,128]{1,0:T(8,128)(2,1)} async-done(((bf16[1024,128]{1,0:T(8,128)(2,1)}), bf16[32768,128]{1,0:T(8,128)(2,1)}) %all-gather.2.cloned.1.call-update) | async-done | bytes 8388624 | tf_op jit(solution)/shard_map/all_gather | solution.py:65
  95.4 0.0 copy-done
  95.4 4.7 %convolution_bitcast_fusion = f32[2048]{0:T(1024)S(1)} fusion(bf16[16,32768]{1,0:T(8,128)(2,1)S(1)} %copy-done, bf16[32768,128]{1,0:T(8,128)(2,1)} %all-gather.2.cloned.1.call-done), kind=kOutput, calls=%fused_computation.11 | convolution fusion | flops 134217728 | bytes 9445376 | tf_op jit(solution)/shard_map/dot_general | solution.py:67
  100.2 0.0 copy-done.2
  100.2 1.0 copy-done.1
  101.2 1.3 convolution_bitcast_fusion.1
  102.5 0.9 broadcast_in_dim.2
  103.4 6.5 %all-to-all-start = ((f32[16,1,4096]{2,1,0:T(1,128)}), f32[16,1,4096]{2,1,0:T(1,128)S(1)}, u32[]{:S(2)}, u32[]{:S(2)}) async-start(f32[16,1,4096]{2,1,0:T(1,128)} %broadcast_in_dim.2), calls=%async_computation | async-start | bytes 524288 | tf_op jit(solution)/shard_map/all_to_all | solution.py:13
  109.9 8.2 %all-to-all-done = f32[16,1,4096]{2,1,0:T(1,128)S(1)} async-done(((f32[16,1,4096]{2,1,0:T(1,128)}), f32[16,1,4096]{2,1,0:T(1,128)S(1)}, u32[]{:S(2)}, u32[]{:S(2)}) %all-to-all-start) | async-done | bytes 262176 | tf_op jit(solution)/shard_map/all_to_all | solution.py:13
  118.2 0.2 reduce_sum.63
  118.4 32.0 %all_gather.7 = f32[512,256]{1,0:T(8,128)S(1)} all-gather(f32[16,256]{1,0:T(8,128)S(1)} %pad_maximum_fusion.1), channel_id=1, replica_groups=mesh['param'=16,'dom'=32] {'dom'}, dimensions={0}, use_global_device_ids=true | all-gather | bytes 540672 | tf_op jit(solution)/shard_map/all_gather | solution.py:33
  150.4 0.7 multiply_reduce_fusion.1
  151.1 0.6 multiply_reduce_fusion.3
  153.0 0.1 multiply_reduce_fusion.2
  153.2 0.4 fusion.13
  153.6 0.2 fusion.8
  153.9 0.2 fusion.7
  154.1 0.0 copy-start.3
  154.1 6.7 %fusion = bf16[16,32768]{1,0:T(8,128)(2,1)} fusion(bf16[32768,128]{1,0:T(8,128)(2,1)} %all-gather.2.cloned.1.call-done, f32[16,128]{1,0:T(8,128)S(1)} %fusion.7), kind=kOutput, calls=%fused_computation.1 | convolution fusion | flops 135268352 | bytes 9445376 | tf_op jit(solution)/shard_map/dot_general | solution.py:53
  160.8 0.0 copy-done.3
  (4 shorter events, 0.0 us)
Async XLA Ops:
  7.2 88.3 %copy-start = (bf16[16,32768]{1,0:T(8,128)(2,1)S(1)}, bf16[16,32768]{1,0:T(8,128)(2,1)}, u32[]{:S(2)}) copy-start(bf16[16,32768]{1,0:T(8,128)(2,1)} %param.4) | copy-start | bytes 3145732
  7.2 88.3 %all-gather.2.cloned.1.call-start = ((), (), s32[]{:S(2)}) async-start(), calls=%async_computation.1 | async-start | bytes 8650752 | tf_op jit(solution)/shard_map/all_gather | solution.py:65
  7.9 92.3 %copy-start.2 = (bf16[16,32768]{1,0:T(8,128)(2,1)S(1)}, bf16[16,32768]{1,0:T(8,128)(2,1)}, u32[]{:S(2)}) copy-start(bf16[16,32768]{1,0:T(8,128)(2,1)} %param.3) | copy-start | bytes 3145732
  95.4 5.8 %copy-start.1 = (bf16[32768,128]{1,0:T(8,128)(2,1)S(1)}, bf16[32768,128]{1,0:T(8,128)(2,1)}, u32[]{:S(2)}) copy-start(bf16[32768,128]{1,0:T(8,128)(2,1)} %all-gather.2.cloned.1.call-done) | copy-start | bytes 25165828
  103.4 14.8 %all-to-all-start = ((f32[16,1,4096]{2,1,0:T(1,128)}), f32[16,1,4096]{2,1,0:T(1,128)S(1)}, u32[]{:S(2)}, u32[]{:S(2)}) async-start(f32[16,1,4096]{2,1,0:T(1,128)} %broadcast_in_dim.2), calls=%async_computation | async-start | bytes 524288 | tf_op jit(solution)/shard_map/all_to_all | solution.py:13
  154.1 6.7 %copy-start.3 = (f32[16,128]{1,0:T(8,128)}, f32[16,128]{1,0:T(8,128)S(1)}, u32[]{:S(2)}) copy-start(f32[16,128]{1,0:T(8,128)S(1)} %fusion.7) | copy-start | bytes 24580
Sparse Core Ops, SparseCore 0:
  10.1 85.2 all-gather.1
where the time goes:
time: 168 us
  waiting for transfers between devices  96.4 us (57%)
  blocking collectives  32 us (19%)
  between operations  15.5 us (9%)
  matrix products  13.6 us (8%)
  starting transfers between devices  6.57 us (4%)
  local copies, waits for them, and re-layouts  1.96 us (1%)
    all_gather x1, waiting for transfers between devices, body(): block_basis = lax.all_gather(basis, 'dom', axis=0, tiled=True)  87.5 us
    all_gather x1, blocking collectives, in_one_piece(): result = lax.all_gather(both, axis, axis=dim, tiled=True)  32 us
    all_to_all x1, waiting for transfers between devices, sent_to_all(): lax.all_to_all(jnp.broadcast_to(array[None], (peers, *array.shape)), axis...  8.23 us
    dot_general x1, matrix products, lift_rows(): lax.dot_general(phi_rows.astype(jnp.bfloat16), basis_rows, (((1,), (1,)),...  6.65 us
    all_to_all x1, starting transfers between devices, sent_to_all(): lax.all_to_all(jnp.broadcast_to(array[None], (peers, *array.shape)), axis...  6.54 us
    dot_general x1, matrix products, body(): partial_s = jnp.dot(scores, block_basis, preferred_element_type=jnp.float32)  4.73 us
  transfers between devices with their start and end apart: 2, of which 2 were waited for; matrix products, arithmetic and copies ran while one was open for 0% of the time, Pallas kernels for 0%

commit v1 on v0

--- a/solution.py
+++ b/solution.py
@@ -62,7 +62,9 @@
 def body(particles, scores, basis):
     rows = particles.shape[0]
     first = lax.axis_index("dom") * rows
-    block_basis = lax.all_gather(basis, "dom", axis=0, tiled=True)
+    block_basis = jnp.concatenate(
+        lax.all_to_all(jnp.stack([basis] * lax.axis_size("dom")), "dom", 0, 0), axis=0
+    )
     partial_c = jnp.dot(particles, block_basis, preferred_element_type=jnp.float32)
     partial_s = jnp.dot(scores, block_basis, preferred_element_type=jnp.float32)
     summed_c, summed_s = in_one((partial_c, partial_s), "param")

time: 168 us -> 451 us (2.68)
  blocking collectives: 32 us -> 417 us
  waiting for transfers between devices: 96.4 us -> 7.96 us
  between operations: 15.5 us -> 2.08 us
    all_to_all x0 -> x1, blocking collectives: none -> 387 us  [body(): lax.all_to_all(jnp.stack([basis] * lax.axis_size('dom')), 'dom', 0, 0)]
    all_gather x1 -> x0, waiting for transfers between devices: 87.5 us -> none  [body(): block_basis = lax.all_gather(basis, 'dom', axis=0, tiled=True)]
  transfers between devices with their start and end apart: 2 -> 1, of which waited for: 2 -> 1; matrix products, arithmetic and copies ran while one was open for 0% -> 0% of each run, Pallas kernels for 0% -> 0%
where the time goes in v1:
time: 451 us
  blocking collectives  417 us (92%)
  matrix products  10 us (2%)
  waiting for transfers between devices  7.96 us (2%)
  starting transfers between devices  6.75 us (1%)
  local copies, waits for them, and re-layouts  5.81 us (1%)
    all_to_all x1, blocking collectives, body(): lax.all_to_all(jnp.stack([basis] * lax.axis_size('dom')), 'dom', 0, 0)  387 us
    all_gather x1, blocking collectives, in_one_piece(): result = lax.all_gather(both, axis, axis=dim, tiled=True)  29.7 us
  transfers between devices with their start and end apart: 1, of which 1 were waited for; matrix products, arithmetic and copies ran while one was open for 0% of the time, Pallas kernels for 0%

profile of v1, /device:TPU:1, one launch (start us, length us, event | category | flops | bytes accessed | tf_op | source)
XLA Modules:
  0.0 450.8 jit_solution(12297169255091266396)
XLA Ops:
  0.6 0.0 copy-start
  0.6 2.9 stack.2
  3.6 386.9 %all_to_all.11 = bf16[32,1024,128]{2,1,0:T(8,128)(2,1)S(1)} all-to-all(bf16[32,1024,128]{2,1,0:T(8,128)(2,1)S(1)} %stack.2), channel_id=1, replica_groups=mesh['param'=16,'dom'=32] {'dom'}, dimensions={0} | all-to-all | bytes 16777216 | tf_op jit(solution)/shard_map/all_to_all | solution.py:66
  390.4 0.0 copy-start.1
  390.4 0.0 copy-done
  390.4 0.0 copy-start.2
  390.4 1.3 convolution_bitcast_fusion
  391.7 2.0 copy-done.1
  393.7 0.0 copy-done.2
  393.7 1.2 convolution_bitcast_fusion.1
  394.9 0.9 broadcast_in_dim.2
  395.8 6.8 %all-to-all-start.1 = ((f32[16,1,4096]{2,1,0:T(1,128)}), f32[16,1,4096]{2,1,0:T(1,128)S(1)}, u32[]{:S(2)}, u32[]{:S(2)}) async-start(f32[16,1,4096]{2,1,0:T(1,128)} %broadcast_in_dim.2), calls=%async_computation.1 | async-start | bytes 524288 | tf_op jit(solution)/shard_map/all_to_all | solution.py:13
  402.6 8.0 %all-to-all-done.1 = f32[16,1,4096]{2,1,0:T(1,128)S(1)} async-done(((f32[16,1,4096]{2,1,0:T(1,128)}), f32[16,1,4096]{2,1,0:T(1,128)S(1)}, u32[]{:S(2)}, u32[]{:S(2)}) %all-to-all-start.1) | async-done | bytes 262176 | tf_op jit(solution)/shard_map/all_to_all | solution.py:13
  410.5 0.2 reduce_sum.63
  410.7 29.7 %all_gather.3 = f32[512,256]{1,0:T(8,128)S(1)} all-gather(f32[16,256]{1,0:T(8,128)S(1)} %pad_maximum_fusion.1), channel_id=1, replica_groups=mesh['param'=16,'dom'=32] {'dom'}, dimensions={0}, use_global_device_ids=true | all-gather | bytes 540672 | tf_op jit(solution)/shard_map/all_gather | solution.py:33
  440.4 0.7 multiply_reduce_fusion.1
  441.1 0.6 multiply_reduce_fusion.3
  443.0 0.1 multiply_reduce_fusion.2
  443.1 0.4 fusion.13
  443.6 0.2 fusion.8
  443.9 0.2 fusion.7
  444.2 0.0 copy-start.3
  444.2 6.7 %fusion = bf16[16,32768]{1,0:T(8,128)(2,1)} fusion(bf16[32768,128]{1,0:T(8,128)(2,1)} %bitcast.20, f32[16,128]{1,0:T(8,128)S(1)} %fusion.7), kind=kOutput, calls=%fused_computation.1 | convolution fusion | flops 135268352 | bytes 9445376 | tf_op jit(solution)/shard_map/dot_general | solution.py:53
  450.8 0.0 copy-done.3
  (3 shorter events, 0.0 us)
Async XLA Ops:
  0.6 389.8 %copy-start = (bf16[16,32768]{1,0:T(8,128)(2,1)S(1)}, bf16[16,32768]{1,0:T(8,128)(2,1)}, u32[]{:S(2)}) copy-start(bf16[16,32768]{1,0:T(8,128)(2,1)} %param.4) | copy-start | bytes 3145732
  390.4 3.2 copy-start.1
  390.4 3.2 copy-start.2
  395.8 14.7 %all-to-all-start.1 = ((f32[16,1,4096]{2,1,0:T(1,128)}), f32[16,1,4096]{2,1,0:T(1,128)S(1)}, u32[]{:S(2)}, u32[]{:S(2)}) async-start(f32[16,1,4096]{2,1,0:T(1,128)} %broadcast_in_dim.2), calls=%async_computation.1 | async-start | bytes 524288 | tf_op jit(solution)/shard_map/all_to_all | solution.py:13
  444.2 6.7 %copy-start.3 = (f32[16,128]{1,0:T(8,128)}, f32[16,128]{1,0:T(8,128)S(1)}, u32[]{:S(2)}) copy-start(f32[16,128]{1,0:T(8,128)S(1)} %fusion.7) | copy-start | bytes 24580
